TPU v7x, 512 devices: a whole 4x8x8 slice. The times are simulated.
512 devices in a mesh: ctx: 64 (over z, y), head: 8 (over x, core).
Axes of the slice: x: 4, y: 8, z: 8, core: 2. Of those that a mesh axis runs over, the one named last changes fastest.
Arguments:
- token_inputs: bfloat16 [32768, 8192], P(('ctx', 'head')), may hold values from -6 to 6
- state_in: bfloat16 [32768, 128], P(('ctx', 'head')), may hold values from -0.059814453 to 0.059814453
- state_out: bfloat16 [32768, 128], P(('ctx', 'head')), may hold values from -0.5 to 0.5
- log_decay: bfloat16 [32768, 128], P(('ctx', 'head')), may hold values from -1 to 0
- token_codes: int32 [32768], P(('ctx', 'head')), may hold values from 0 to 63
- level_table: bfloat16 [64, 1408], replicated, may hold values from 0.099609375 to 1
- skip_gain: float32 [128], replicated, may hold values from 0.2 to 1
Outputs:
- mixed_output: bfloat16 [32768, 8192], P(('ctx', 'head'))
All inputs are finite; a program needn't handle non-finite values.
Results may differ from a plain program's by a relative error of at most 0.009.
Values may be sent and summed in bfloat16 or wider, within the bound.
A program may use at most 64 MiB of HBM per device.

v0:
```python
import jax
import jax.numpy as jnp
from jax import lax
from jax.sharding import PartitionSpec as P

COUNT_OF_HEADS = 128
HEAD_DIM = 64
SPAN = 64
LEVELS = 11


def swapped(x, axis, apart):
    return lax.ppermute(x, axis, [(i, i ^ 1 << apart) for i in range(lax.axis_size(axis))])


def look_up(token_codes, weight_table):
    one_hot = (
        token_codes[:, None] == jnp.arange(weight_table.shape[0], dtype=jnp.int32)[None, :]
    ).astype(jnp.bfloat16)
    return jnp.dot(one_hot, weight_table, preferred_element_type=jnp.float32).astype(jnp.bfloat16)


def level_onehot(spans, levels):
    span_ids = jnp.arange(spans, dtype=jnp.int32)
    xored = jnp.bitwise_xor(span_ids[:, None], span_ids[None, :])
    level_ids = jnp.zeros((spans, spans), jnp.int32)
    for level_bit in range(max(spans.bit_length() - 1, 0)):
        level_ids = level_ids + (xored >= 1 << level_bit).astype(jnp.int32)
    return (level_ids[:, :, None] == jnp.arange(levels, dtype=jnp.int32)[None, None, :]).astype(
        jnp.float32
    )


def head_local(scores, head_input, head_weights, head_running, onehot, span):
    block_rows = head_input.shape[0]
    spans = block_rows // span
    weight_blocks = head_weights.astype(jnp.float32).reshape(spans, span, -1)
    pair_weights = jnp.einsum(
        "iql,ijl->iqj", weight_blocks, onehot, precision=lax.Precision.HIGHEST
    )
    row_weights = jnp.broadcast_to(
        pair_weights.reshape(block_rows, spans, 1), (block_rows, spans, span)
    ).reshape(block_rows, block_rows)
    position = jnp.arange(block_rows)
    causal = position[:, None] >= position[None, :]
    log_gap = jnp.where(causal, head_running[:, None] - head_running[None, :], 0.0)
    decay_factor = jnp.where(causal, jnp.exp(log_gap), 0.0)
    weight = (row_weights * decay_factor * scores).astype(jnp.bfloat16)
    return jnp.dot(weight, head_input, preferred_element_type=jnp.float32)


def head_state(head_input, head_running, state_in):
    carried = jnp.exp(head_running[-1] - head_running)[:, None] * head_input.astype(jnp.float32)
    return jnp.einsum(
        "tn,tp->np", state_in, carried.astype(jnp.bfloat16), preferred_element_type=jnp.float32
    )


def finish(
    local_part,
    head_input,
    head_weights,
    head_running,
    state_out,
    bucket_states,
    skip_value,
    span_bits,
    ctx_bits,
):
    reached = jnp.einsum(
        "tn,mnp->tmp", state_out, bucket_states, preferred_element_type=jnp.float32
    )
    factors = (
        head_weights[:, span_bits + 1 : span_bits + 1 + ctx_bits].astype(jnp.float32)
        * jnp.exp(head_running)[:, None]
    )
    cross_part = jnp.sum(factors[:, :, None] * reached, axis=1)
    return (local_part + cross_part + skip_value * head_input.astype(jnp.float32)).astype(
        jnp.bfloat16
    )


def on_device(token_inputs, state_in, state_out, log_decay, token_codes, level_table, skip_gain):
    head_ways = lax.axis_size("head")
    local_heads = COUNT_OF_HEADS // head_ways
    offset = lax.axis_index("head")
    weights_seq = look_up(token_codes, level_table)
    moved_rows, moved_weights, moved_decay = (
        lax.all_to_all(token_inputs, "head", split_axis=1, concat_axis=0, tiled=True),
        lax.all_to_all(weights_seq, "head", split_axis=1, concat_axis=0, tiled=True),
        lax.all_to_all(log_decay, "head", split_axis=1, concat_axis=0, tiled=True),
    )
    in_all, out_all = (
        lax.all_gather(state_in, "head", axis=0, tiled=True),
        lax.all_gather(state_out, "head", axis=0, tiled=True),
    )
    block_rows = moved_rows.shape[0]
    spans = block_rows // SPAN
    span_bits = spans.bit_length() - 1
    input_all = moved_rows.reshape(block_rows, local_heads, HEAD_DIM)
    weights_all = moved_weights.reshape(block_rows, local_heads, LEVELS)
    running = jnp.cumsum(moved_decay.astype(jnp.float32), axis=0)
    onehot = level_onehot(spans, LEVELS)
    scores = jnp.einsum("tn,sn->ts", out_all, in_all, preferred_element_type=jnp.float32)

    def first_pass(head_index):
        head_input = input_all[:, head_index]
        head_running = running[:, head_index]
        local_part = head_local(
            scores, head_input, weights_all[:, head_index], head_running, onehot, SPAN
        )
        return (local_part, head_state(head_input, head_running, in_all))

    local_all, states = lax.map(first_pass, jnp.arange(local_heads))
    summary = states
    summary_decay = running[-1]
    inside = jnp.zeros_like(summary_decay)
    device = lax.axis_index("ctx")
    ctx_bits = lax.axis_size("ctx").bit_length() - 1
    buckets = []
    for level_bit in range(ctx_bits):
        partner, partner_decay = (
            swapped(summary.astype(jnp.bfloat16), "ctx", level_bit).astype(summary.dtype),
            swapped(summary_decay.astype(jnp.bfloat16), "ctx", level_bit).astype(
                summary_decay.dtype
            ),
        )
        is_upper = device >> level_bit & 1 == 1
        buckets.append(
            jnp.where(is_upper, partner * jnp.exp(inside)[:, None, None], 0.0).astype(jnp.bfloat16)
        )
        summary = jnp.where(
            is_upper,
            partner * jnp.exp(summary_decay)[:, None, None] + summary,
            summary * jnp.exp(partner_decay)[:, None, None] + partner,
        )
        inside = jnp.where(is_upper, inside + partner_decay, inside)
        summary_decay = summary_decay + partner_decay
    bucket_stack = jnp.stack(buckets, axis=0)
    gains = lax.dynamic_slice_in_dim(skip_gain, offset * local_heads, local_heads, 0)

    def second_pass(head_index):
        return finish(
            local_all[head_index],
            input_all[:, head_index],
            weights_all[:, head_index],
            running[:, head_index],
            out_all,
            bucket_stack[:, head_index],
            gains[head_index],
            span_bits,
            ctx_bits,
        )

    mixed_rows = lax.map(second_pass, jnp.arange(local_heads))
    merged = jnp.moveaxis(mixed_rows, 0, 1).reshape(block_rows, local_heads * HEAD_DIM)
    return lax.all_to_all(merged, "head", split_axis=0, concat_axis=1, tiled=True)


def solution(mesh):
    return jax.shard_map(
        on_device,
        mesh=mesh,
        in_specs=(
            P(("ctx", "head"), None),
            P(("ctx", "head"), None),
            P(("ctx", "head"), None),
            P(("ctx", "head"), None),
            P(("ctx", "head")),
            P(),
            P(),
        ),
        out_specs=P(("ctx", "head"), None),
        check_vma=False,
    )
```

profile of v0, /device:TPU:1, one launch (start us, length us, event | category | flops | bytes accessed | tf_op | source)
XLA Modules:
  0.0 465.8 jit_solution(6821224827247671395)
XLA Ops:
  1.6 10.1 %all-to-all-start.1 = ((bf16[8,2,512]{2,1,0:T(2,128)(2,1)}), bf16[8,2,512]{2,1,0:T(2,128)(2,1)S(1)}, u32[]{:S(2)}, u32[]{:S(2)}) async-start(bf16[8,2,512]{2,1,0:T(2,128)(2,1)} %reshape.216), calls=%async_computation.1 | async-start | bytes 32768 | tf_op jit(solution)/shard_map/all_to_all | solution.py:91
  11.7 13.7 %all_gather.6 = bf16[512,128]{1,0:T(8,128)(2,1)S(1)} all-gather(bf16[64,128]{1,0:T(8,128)(2,1)} %param.13), channel_id=1, replica_groups=mesh['ctx'=64,'head'=8] {'head'}, dimensions={0}, use_global_device_ids=true | all-gather | bytes 147456 | tf_op jit(solution)/shard_map/all_gather | solution.py:95
  25.4 12.9 %all_gather.7 = bf16[512,128]{1,0:T(8,128)(2,1)S(1)} all-gather(bf16[64,128]{1,0:T(8,128)(2,1)} %param.12), channel_id=1, replica_groups=mesh['ctx'=64,'head'=8] {'head'}, dimensions={0}, use_global_device_ids=true | all-gather | bytes 147456 | tf_op jit(solution)/shard_map/all_gather | solution.py:94
  41.2 3.8 all-to-all-start
  46.6 4.9 %all-to-all-done = bf16[64,8,176]{2,0,1:T(8,128)(2,1)S(1)} async-done(((bf16[64,8,176]{2,0,1:T(8,128)(2,1)}), bf16[64,8,176]{2,0,1:T(8,128)(2,1)S(1)}, u32[]{:S(2)}, u32[]{:S(2)}) %all-to-all-start) | async-done | bytes 180256 | tf_op jit(solution)/shard_map/all_to_all | solution.py:90
  51.5 4.5 all-to-all-start.2
  58.2 2.7 collective-permute-done.1
  62.8 3.6 collective-permute-done.3
  66.4 3.1 collective-permute-start.5
  69.5 5.1 %collective-permute-done.5 = bf16[16]{0:T(256)(128)(2,1)S(1)} collective-permute-done((bf16[16]{0:T(256)(128)(2,1)S(1)}, bf16[16]{0:T(256)(128)(2,1)S(1)}, u32[]{:S(2)}, u32[]{:S(2)}) %collective-permute-start.5) | collective-permute-done | bytes 64 | tf_op jit(solution)/shard_map/ppermute | solution.py:13
  78.7 2.9 reshape.198
  84.2 159.0 %while.26 = (s32[]{:T(128)}, f32[16,512,64]{1,2,0:T(8,128)}, f32[16,128,64]{1,2,0:T(8,128)}, s32[16]{0:T(128)S(1)}, bf16[512,16,11]{0,2,1:T(8,128)(2,1)}, /*inde...) while((s32[]{:T(128)}, f32[16,512,64]{1,2,0:T(8,128)}, ...), condition=%wide.region_3.4_spmd.clone.clone, body=%wide.region_2.3_spmd.clone.sunk.clone | while | flops 44419972 | bytes 2703819 | solution.py:114
  246.3 4.9 %collective-permute-start.9 = (bf16[16]{0:T(256)(128)(2,1)S(1)}, bf16[16]{0:T(256)(128)(2,1)S(1)}, u32[]{:S(2)}, u32[]{:S(2)}) collective-permute-start(bf16[16]{0:T(256)(128)(2,1)S(1)} %get-tuple-element.258), channel_id=1, source_target_pairs={{0,128},{8,136},{16,144},{24,152},{32,160},{40,168},{48,176},{56,1... | collective-permute-start | bytes 104 | tf_op jit(solution)/shard_map/ppermute | solution.py:13
  253.4 4.2 collective-permute-start.2
  257.6 10.5 %collective-permute-done.2 = bf16[16,128,64]{1,2,0:T(8,128)(2,1)S(1)} collective-permute-done((bf16[16,128,64]{1,2,0:T(8,128)(2,1)S(1)}, bf16[16,128,64]{1,2,0:T(8,128)(2,1)S(1)}, u32[]{:S(2)}, u32[]{:S(2)}) %collective-permute-start.2) | collective-permute-done | bytes 262176 | tf_op jit(solution)/shard_map/ppermute | solution.py:13
  268.4 6.6 %collective-permute-start.4 = (bf16[16,128,64]{1,2,0:T(8,128)(2,1)S(1)}, bf16[16,128,64]{1,2,0:T(8,128)(2,1)S(1)}, u32[]{:S(2)}, u32[]{:S(2)}) collective-permute-start(bf16[16,128,64]{1,2,0:T(8,128)(2,1)S(1)} %fusion.67), channel_id=1, source_target_pairs={{0,32},{8,40},{16,48},{24,56},{32,0},{40,8},{48,16},{56,24},{64,96... | collective-permute-start | bytes 786440 | tf_op jit(solution)/shard_map/ppermute | solution.py:13
  275.1 11.6 %collective-permute-done.4 = bf16[16,128,64]{1,2,0:T(8,128)(2,1)S(1)} collective-permute-done((bf16[16,128,64]{1,2,0:T(8,128)(2,1)S(1)}, bf16[16,128,64]{1,2,0:T(8,128)(2,1)S(1)}, u32[]{:S(2)}, u32[]{:S(2)}) %collective-permute-start.4) | collective-permute-done | bytes 262176 | tf_op jit(solution)/shard_map/ppermute | solution.py:13
  289.1 5.8 %collective-permute-done.6 = bf16[16,128,64]{1,2,0:T(8,128)(2,1)S(1)} collective-permute-done((bf16[16,128,64]{1,2,0:T(8,128)(2,1)S(1)}, bf16[16,128,64]{1,2,0:T(8,128)(2,1)S(1)}, u32[]{:S(2)}, u32[]{:S(2)}) %collective-permute-start.6) | collective-permute-done | bytes 262176 | tf_op jit(solution)/shard_map/ppermute | solution.py:13
  295.1 3.1 collective-permute-start.8
  298.6 13.1 %collective-permute-done.8 = bf16[16,128,64]{1,2,0:T(8,128)(2,1)S(1)} collective-permute-done((bf16[16,128,64]{1,2,0:T(8,128)(2,1)S(1)}, bf16[16,128,64]{1,2,0:T(8,128)(2,1)S(1)}, u32[]{:S(2)}, u32[]{:S(2)}) %collective-permute-start.8) | collective-permute-done | bytes 262176 | tf_op jit(solution)/shard_map/ppermute | solution.py:13
  312.0 4.5 collective-permute-start.10
  316.9 14.3 %collective-permute-done.10 = bf16[16,128,64]{1,2,0:T(8,128)(2,1)S(1)} collective-permute-done((bf16[16,128,64]{1,2,0:T(8,128)(2,1)S(1)}, bf16[16,128,64]{1,2,0:T(8,128)(2,1)S(1)}, u32[]{:S(2)}, u32[]{:S(2)}) %collective-permute-start.10) | collective-permute-done | bytes 262176 | tf_op jit(solution)/shard_map/ppermute | solution.py:13
  332.5 111.8 %while.25 = (s32[]{:T(128)}, bf16[16,512,64]{1,2,0:T(8,128)(2,1)S(1)}, s32[16]{0:T(128)S(1)}, f32[16,512,64]{1,2,0:T(8,128)}, bf16[512,16,11]{0,2,1:T(8,128)(2,1...) while((s32[]{:T(128)}, ...), condition=%wide.region_6.7_spmd.clone, body=%wide.region_4.6_spmd.sunk.clone | while | flops 50862084 | bytes 813239 | solution.py:155
  446.9 17.8 %all_to_all.64 = bf16[8,64,1024]{2,1,0:T(8,128)(2,1)S(1)} all-to-all(bf16[8,64,1024]{2,1,0:T(8,128)(2,1)S(1)} %copy.58), channel_id=1, replica_groups=mesh['ctx'=64,'head'=8] {'head'}, dimensions={0} | all-to-all | bytes 2097152 | tf_op jit(solution)/shard_map/all_to_all | solution.py:157
  (433 shorter events, 237.5 us)
Async XLA Ops:
  0.0 38.6 %copy-start = (bf16[64,1408]{1,0:T(8,128)(2,1)S(1)}, bf16[64,1408]{1,0:T(8,128)(2,1)}, u32[]{:S(2)}) copy-start(bf16[64,1408]{1,0:T(8,128)(2,1)} %param.16) | copy-start | bytes 540676
  0.0 38.6 %copy-start.7 = (s32[64]{0:T(128)S(1)}, s32[64]{0:T(128)}, u32[]{:S(2)}) copy-start(s32[64]{0:T(128)} %param.15) | copy-start | bytes 772
  0.0 38.9 %copy-start.3 = (bf16[64,8192]{1,0:T(8,128)(2,1)S(1)}, bf16[64,8192]{1,0:T(8,128)(2,1)}, u32[]{:S(2)}) copy-start(bf16[64,8192]{1,0:T(8,128)(2,1)} %param.11) | copy-start | bytes 3145732
  1.6 39.5 %all-to-all-start.1 = ((bf16[8,2,512]{2,1,0:T(2,128)(2,1)}), bf16[8,2,512]{2,1,0:T(2,128)(2,1)S(1)}, u32[]{:S(2)}, u32[]{:S(2)}) async-start(bf16[8,2,512]{2,1,0:T(2,128)(2,1)} %reshape.216), calls=%async_computation.1 | async-start | bytes 32768 | tf_op jit(solution)/shard_map/all_to_all | solution.py:91
  25.4 13.0 %copy-start.4 = (bf16[512,128]{1,0:T(8,128)(2,1)}, bf16[512,128]{1,0:T(8,128)(2,1)S(1)}, u32[]{:S(2)}) copy-start(bf16[512,128]{1,0:T(8,128)(2,1)S(1)} %all_gather.6) | copy-start | bytes 393220
  41.2 10.3 %all-to-all-start = ((bf16[64,8,176]{2,0,1:T(8,128)(2,1)}), bf16[64,8,176]{2,0,1:T(8,128)(2,1)S(1)}, u32[]{:S(2)}, u32[]{:S(2)}) async-start(bf16[64,8,176]{2,0,1:T(8,128)(2,1)} %copy.44), calls=%async_computation | async-start | bytes 524288 | tf_op jit(solution)/shard_map/all_to_all | solution.py:90
  51.5 26.3 %all-to-all-start.2 = ((bf16[64,8,1024]{2,0,1:T(8,128)(2,1)}), bf16[64,8,1024]{2,0,1:T(8,128)(2,1)S(1)}, u32[]{:S(2)}, u32[]{:S(2)}) async-start(bf16[64,8,1024]{2,0,1:T(8,128)(2,1)} %bitcast.122), calls=%async_computation.2 | async-start | bytes 2097152 | tf_op jit(solution)/shard_map/all_to_all | solution.py:89
  56.2 4.6 collective-permute-start.1
  60.9 5.5 %collective-permute-start.3 = (bf16[16]{0:T(256)(128)(2,1)S(1)}, bf16[16]{0:T(256)(128)(2,1)S(1)}, u32[]{:S(2)}, u32[]{:S(2)}) collective-permute-start(bf16[16]{0:T(256)(128)(2,1)S(1)} %fusion.63), channel_id=1, source_target_pairs={{0,16},{8,24},{16,0},{24,8},{32,48},{40,56},{48,32},{56,40},{64,80... | collective-permute-start | bytes 104 | tf_op jit(solution)/shard_map/ppermute | solution.py:13
  66.4 8.2 %collective-permute-start.5 = (bf16[16]{0:T(256)(128)(2,1)S(1)}, bf16[16]{0:T(256)(128)(2,1)S(1)}, u32[]{:S(2)}, u32[]{:S(2)}) collective-permute-start(bf16[16]{0:T(256)(128)(2,1)S(1)} %convert_element_type.176), channel_id=1, source_target_pairs={{0,32},{8,40},{16,48},{24,56},{32,0},{40,8},{48,16},{56,24},{64,96... | collective-permute-start | bytes 104 | tf_op jit(solution)/shard_map/ppermute | solution.py:13
  74.6 171.7 %collective-permute-start.7 = (bf16[16]{0:T(256)(128)(2,1)S(1)}, bf16[16]{0:T(256)(128)(2,1)S(1)}, u32[]{:S(2)}, u32[]{:S(2)}) collective-permute-start(bf16[16]{0:T(256)(128)(2,1)S(1)} %convert_element_type.181), channel_id=1, source_target_pairs={{0,64},{8,72},{16,80},{24,88},{32,96},{40,104},{48,112},{56,120},{... | collective-permute-start | bytes 104 | tf_op jit(solution)/shard_map/ppermute | solution.py:13
  77.8 1.0 copy-start.2
  243.2 24.9 %copy-start.1 = (f32[16,128,64]{1,2,0:T(8,128)S(1)}, f32[16,128,64]{1,2,0:T(8,128)}, u32[]{:S(2)}) copy-start(f32[16,128,64]{1,2,0:T(8,128)} %get-tuple-element.111) | copy-start | bytes 1572868
  243.2 31.8 %copy-start.8 = (f32[128]{0:T(128)S(1)}, f32[128]{0:T(128)}, u32[]{:S(2)}) copy-start(f32[128]{0:T(128)} %param.17) | copy-start | bytes 1540
  244.3 7.8 %collective-permute-start = (bf16[16,128,64]{1,2,0:T(8,128)(2,1)S(1)}, bf16[16,128,64]{1,2,0:T(8,128)(2,1)S(1)}, u32[]{:S(2)}, u32[]{:S(2)}) collective-permute-start(bf16[16,128,64]{1,2,0:T(8,128)(2,1)S(1)} %convert_element_type.163), channel_id=1, source_target_pairs={{0,8},{8,0},{16,24},{24,16},{32,40},{40,32},{48,56},{56,48},{64,72... | collective-permute-start | bytes 786440 | tf_op jit(solution)/shard_map/ppermute | solution.py:13
  246.3 5.8 %collective-permute-start.9 = (bf16[16]{0:T(256)(128)(2,1)S(1)}, bf16[16]{0:T(256)(128)(2,1)S(1)}, u32[]{:S(2)}, u32[]{:S(2)}) collective-permute-start(bf16[16]{0:T(256)(128)(2,1)S(1)} %get-tuple-element.258), channel_id=1, source_target_pairs={{0,128},{8,136},{16,144},{24,152},{32,160},{40,168},{48,176},{56,1... | collective-permute-start | bytes 104 | tf_op jit(solution)/shard_map/ppermute | solution.py:13
  253.4 14.7 %collective-permute-start.2 = (bf16[16,128,64]{1,2,0:T(8,128)(2,1)S(1)}, bf16[16,128,64]{1,2,0:T(8,128)(2,1)S(1)}, u32[]{:S(2)}, u32[]{:S(2)}) collective-permute-start(bf16[16,128,64]{1,2,0:T(8,128)(2,1)S(1)} %fusion.68), channel_id=1, source_target_pairs={{0,16},{8,24},{16,0},{24,8},{32,48},{40,56},{48,32},{56,40},{64,80... | collective-permute-start | bytes 786440 | tf_op jit(solution)/shard_map/ppermute | solution.py:13
  268.4 18.2 %collective-permute-start.4 = (bf16[16,128,64]{1,2,0:T(8,128)(2,1)S(1)}, bf16[16,128,64]{1,2,0:T(8,128)(2,1)S(1)}, u32[]{:S(2)}, u32[]{:S(2)}) collective-permute-start(bf16[16,128,64]{1,2,0:T(8,128)(2,1)S(1)} %fusion.67), channel_id=1, source_target_pairs={{0,32},{8,40},{16,48},{24,56},{32,0},{40,8},{48,16},{56,24},{64,96... | collective-permute-start | bytes 786440 | tf_op jit(solution)/shard_map/ppermute | solution.py:13
  287.1 7.9 %collective-permute-start.6 = (bf16[16,128,64]{1,2,0:T(8,128)(2,1)S(1)}, bf16[16,128,64]{1,2,0:T(8,128)(2,1)S(1)}, u32[]{:S(2)}, u32[]{:S(2)}) collective-permute-start(bf16[16,128,64]{1,2,0:T(8,128)(2,1)S(1)} %get-tuple-element.253), channel_id=1, source_target_pairs={{0,64},{8,72},{16,80},{24,88},{32,96},{40,104},{48,112},{56,120},{... | collective-permute-start | bytes 786440 | tf_op jit(solution)/shard_map/ppermute | solution.py:13
  295.1 16.6 %collective-permute-start.8 = (bf16[16,128,64]{1,2,0:T(8,128)(2,1)S(1)}, bf16[16,128,64]{1,2,0:T(8,128)(2,1)S(1)}, u32[]{:S(2)}, u32[]{:S(2)}) collective-permute-start(bf16[16,128,64]{1,2,0:T(8,128)(2,1)S(1)} %fusion.66), channel_id=1, source_target_pairs={{0,128},{8,136},{16,144},{24,152},{32,160},{40,168},{48,176},{56,1... | collective-permute-start | bytes 786440 | tf_op jit(solution)/shard_map/ppermute | solution.py:13
  298.6 33.9 %copy-start.5 = (bf16[512,128]{1,0:T(8,128)(2,1)S(1)}, bf16[512,128]{1,0:T(8,128)(2,1)}, u32[]{:S(2)}) copy-start(bf16[512,128]{1,0:T(8,128)(2,1)} %copy-done.4) | copy-start | bytes 393220
  312.0 19.1 %collective-permute-start.10 = (bf16[16,128,64]{1,2,0:T(8,128)(2,1)S(1)}, bf16[16,128,64]{1,2,0:T(8,128)(2,1)S(1)}, u32[]{:S(2)}, u32[]{:S(2)}) collective-permute-start(bf16[16,128,64]{1,2,0:T(8,128)(2,1)S(1)} %fusion.42), channel_id=1, source_target_pairs={{0,256},{8,264},{16,272},{24,280},{32,288},{40,296},{48,304},{56,3... | collective-permute-start | bytes 786440 | tf_op jit(solution)/shard_map/ppermute | solution.py:13
  331.4 1.2 copy-start.6
where the time goes:
time: 472 us; the launch traced here: 466 us
  local copies, waits for them, and re-layouts  95.3 us (20%)
  matrix products  75.6 us (16%)
  waiting for transfers between devices  72.5 us (15%)
  loops' own time  64.2 us (14%)
  other arithmetic  59 us (12%)
  starting transfers between devices  54.4 us (12%)
  blocking collectives  44.4 us (9%)
    ppermute x11, waiting for transfers between devices, swapped(): lax.ppermute(x, axis, [(i, i ^ 1 << apart) for i in range(lax.axis_size(a...  67.5 us
    ppermute x11, starting transfers between devices, swapped(): lax.ppermute(x, axis, [(i, i ^ 1 << apart) for i in range(lax.axis_size(a...  36 us
    another operation x1, loops' own time, on_device(): mixed_rows = lax.map(second_pass, jnp.arange(local_heads))  33.8 us
    another operation x1, loops' own time, on_device(): local_all, states = lax.map(first_pass, jnp.arange(local_heads))  30.4 us
    dot_general x16, matrix products, head_local(): return jnp.dot(weight, head_input, preferred_element_type=jnp.float32)  27.3 us
    dynamic_update_slice x16, other arithmetic, on_device(): mixed_rows = lax.map(second_pass, jnp.arange(local_heads))  26 us
    dot_general x16, matrix products, head_state(): jnp.einsum('tn,tp->np', state_in, carried.astype(jnp.bfloat16), preferred...  25.6 us
    dynamic_slice x32, local copies, waits for them, and re-layouts, on_device(): local_all, states = lax.map(first_pass, jnp.arange(local_heads))  20.8 us
  transfers between devices with their start and end apart: 14, of which 10 were waited for; matrix products, arithmetic and copies ran while one was open for 30% of the time, Pallas kernels for 0%

commit v1 on v0

--- a/solution.py
+++ b/solution.py
@@ -91,7 +91,9 @@
         lax.all_to_all(log_decay, "head", split_axis=1, concat_axis=0, tiled=True),
     )
     in_all, out_all = (
-        lax.all_gather(state_in, "head", axis=0, tiled=True),
+        jnp.concatenate(
+            lax.all_to_all(jnp.stack([state_in] * lax.axis_size("head")), "head", 0, 0), axis=0
+        ),
         lax.all_gather(state_out, "head", axis=0, tiled=True),
     )
     block_rows = moved_rows.shape[0]

time: 472 us -> 458 us (0.970)
  starting transfers between devices: 54.4 us -> 65 us
  waiting for transfers between devices: 72.5 us -> 63.9 us
  blocking collectives: 44.4 us -> 36.9 us
  loops' own time: 64.2 us -> 58.8 us
    all_gather x1 -> x0, blocking collectives: 12.9 us -> none  [on_device(): lax.all_gather(state_in, 'head', axis=0, tiled=True)]
    ppermute x11, waiting for transfers between devices: 67.5 us -> 55.9 us  [swapped(): lax.ppermute(x, axis, [(i, i ^ 1 << apart) for i in range(lax.axis_size(a...]
    ppermute x11, starting transfers between devices: 36 us -> 42.4 us  [swapped(): lax.ppermute(x, axis, [(i, i ^ 1 << apart) for i in range(lax.axis_size(a...]
    another operation x1, loops' own time: 33.8 us -> 27.9 us  [on_device(): mixed_rows = lax.map(second_pass, jnp.arange(local_heads))]
    all_to_all x1, blocking collectives: 17.8 us -> 23.2 us  [on_device(): lax.all_to_all(merged, 'head', split_axis=0, concat_axis=1, tiled=True)]
  transfers between devices with their start and end apart: 14 -> 15, of which waited for: 10 -> 10; matrix products, arithmetic and copies ran while one was open for 30% -> 31% of each run, Pallas kernels for 0% -> 0%
where the time goes in v1:
time: 458 us; the launch traced here: 451 us
  local copies, waits for them, and re-layouts  92.6 us (20%)
  matrix products  76.4 us (17%)
  starting transfers between devices  65 us (14%)
  waiting for transfers between devices  63.9 us (14%)
  loops' own time  58.8 us (13%)
  other arithmetic  57.4 us (13%)
  blocking collectives  36.9 us (8%)
    ppermute x11, waiting for transfers between devices, swapped(): lax.ppermute(x, axis, [(i, i ^ 1 << apart) for i in range(lax.axis_size(a...  55.9 us
    ppermute x11, starting transfers between devices, swapped(): lax.ppermute(x, axis, [(i, i ^ 1 << apart) for i in range(lax.axis_size(a...  42.4 us
    another operation x1, loops' own time, on_device(): local_all, states = lax.map(first_pass, jnp.arange(local_heads))  31 us
    another operation x1, loops' own time, on_device(): mixed_rows = lax.map(second_pass, jnp.arange(local_heads))  27.9 us
    dot_general x16, matrix products, head_local(): return jnp.dot(weight, head_input, preferred_element_type=jnp.float32)  27.3 us
    dot_general x16, matrix products, head_state(): jnp.einsum('tn,tp->np', state_in, carried.astype(jnp.bfloat16), preferred...  25.7 us
    dynamic_update_slice x16, other arithmetic, on_device(): mixed_rows = lax.map(second_pass, jnp.arange(local_heads))  24 us
    all_to_all x1, blocking collectives, on_device(): lax.all_to_all(merged, 'head', split_axis=0, concat_axis=1, tiled=True)  23.2 us
  transfers between devices with their start and end apart: 15, of which 10 were waited for; matrix products, arithmetic and copies ran while one was open for 31% of the time, Pallas kernels for 0%

profile of v1, /device:TPU:1, one launch (start us, length us, event | category | flops | bytes accessed | tf_op | source)
XLA Modules:
  0.0 451.3 jit_solution(16849872323951206448)
XLA Ops:
  1.6 10.1 %all-to-all-start.1 = ((bf16[8,2,512]{2,1,0:T(2,128)(2,1)}), bf16[8,2,512]{2,1,0:T(2,128)(2,1)S(1)}, u32[]{:S(2)}, u32[]{:S(2)}) async-start(bf16[8,2,512]{2,1,0:T(2,128)(2,1)} %reshape.222), calls=%async_computation.1 | async-start | bytes 32768 | tf_op jit(solution)/shard_map/all_to_all | solution.py:91
  12.6 13.7 %all_gather.3 = bf16[512,128]{1,0:T(8,128)(2,1)S(1)} all-gather(bf16[64,128]{1,0:T(8,128)(2,1)} %param.13), channel_id=1, replica_groups=mesh['ctx'=64,'head'=8] {'head'}, dimensions={0}, use_global_device_ids=true | all-gather | bytes 147456 | tf_op jit(solution)/shard_map/all_gather | solution.py:97
  30.4 3.8 all-to-all-start.2
  35.8 3.7 all-to-all-done.2
  39.5 4.2 all-to-all-start
  45.9 4.3 all-to-all-done
  50.2 4.5 all-to-all-start.3
  56.6 3.6 collective-permute-done.3
  60.2 3.1 collective-permute-start.5
  63.4 5.1 %collective-permute-done.5 = bf16[16]{0:T(256)(128)(2,1)S(1)} collective-permute-done((bf16[16]{0:T(256)(128)(2,1)S(1)}, bf16[16]{0:T(256)(128)(2,1)S(1)}, u32[]{:S(2)}, u32[]{:S(2)}) %collective-permute-start.5) | collective-permute-done | bytes 64 | tf_op jit(solution)/shard_map/ppermute | solution.py:13
  78.3 158.3 %while.26 = (s32[]{:T(128)}, f32[16,512,64]{1,2,0:T(8,128)}, f32[16,128,64]{1,2,0:T(8,128)}, s32[16]{0:T(128)S(1)}, bf16[512,16,11]{0,2,1:T(8,128)(2,1)}, /*inde...) while((s32[]{:T(128)}, f32[16,512,64]{1,2,0:T(8,128)}, ...), condition=%wide.region_3.4_spmd.clone.clone, body=%wide.region_2.3_spmd.clone.sunk.clone | while | flops 44419972 | bytes 2703819 | solution.py:116
  239.8 4.9 %collective-permute-start.9 = (bf16[16]{0:T(256)(128)(2,1)S(1)}, bf16[16]{0:T(256)(128)(2,1)S(1)}, u32[]{:S(2)}, u32[]{:S(2)}) collective-permute-start(bf16[16]{0:T(256)(128)(2,1)S(1)} %get-tuple-element.258), channel_id=1, source_target_pairs={{0,128},{8,136},{16,144},{24,152},{32,160},{40,168},{48,176},{56,1... | collective-permute-start | bytes 104 | tf_op jit(solution)/shard_map/ppermute | solution.py:13
  246.9 4.2 collective-permute-start.2
  251.1 11.3 %collective-permute-done.2 = bf16[16,128,64]{1,2,0:T(8,128)(2,1)S(1)} collective-permute-done((bf16[16,128,64]{1,2,0:T(8,128)(2,1)S(1)}, bf16[16,128,64]{1,2,0:T(8,128)(2,1)S(1)}, u32[]{:S(2)}, u32[]{:S(2)}) %collective-permute-start.2) | collective-permute-done | bytes 262176 | tf_op jit(solution)/shard_map/ppermute | solution.py:13
  262.7 6.5 %collective-permute-start.4 = (bf16[16,128,64]{1,2,0:T(8,128)(2,1)S(1)}, bf16[16,128,64]{1,2,0:T(8,128)(2,1)S(1)}, u32[]{:S(2)}, u32[]{:S(2)}) collective-permute-start(bf16[16,128,64]{1,2,0:T(8,128)(2,1)S(1)} %fusion.67), channel_id=1, source_target_pairs={{0,32},{8,40},{16,48},{24,56},{32,0},{40,8},{48,16},{56,24},{64,96... | collective-permute-start | bytes 786440 | tf_op jit(solution)/shard_map/ppermute | solution.py:13
  269.4 11.5 %collective-permute-done.4 = bf16[16,128,64]{1,2,0:T(8,128)(2,1)S(1)} collective-permute-done((bf16[16,128,64]{1,2,0:T(8,128)(2,1)S(1)}, bf16[16,128,64]{1,2,0:T(8,128)(2,1)S(1)}, u32[]{:S(2)}, u32[]{:S(2)}) %collective-permute-start.4) | collective-permute-done | bytes 262176 | tf_op jit(solution)/shard_map/ppermute | solution.py:13
  281.3 3.2 collective-permute-start.6
  284.6 4.4 collective-permute-done.6
  289.2 4.0 collective-permute-start.8
  293.6 10.8 %collective-permute-done.8 = bf16[16,128,64]{1,2,0:T(8,128)(2,1)S(1)} collective-permute-done((bf16[16,128,64]{1,2,0:T(8,128)(2,1)S(1)}, bf16[16,128,64]{1,2,0:T(8,128)(2,1)S(1)}, u32[]{:S(2)}, u32[]{:S(2)}) %collective-permute-start.8) | collective-permute-done | bytes 262176 | tf_op jit(solution)/shard_map/ppermute | solution.py:13
  304.7 8.8 %collective-permute-start.10 = (bf16[16,128,64]{1,2,0:T(8,128)(2,1)S(1)}, bf16[16,128,64]{1,2,0:T(8,128)(2,1)S(1)}, u32[]{:S(2)}, u32[]{:S(2)}) collective-permute-start(bf16[16,128,64]{1,2,0:T(8,128)(2,1)S(1)} %fusion.42), channel_id=1, source_target_pairs={{0,256},{8,264},{16,272},{24,280},{32,288},{40,296},{48,304},{56,3... | collective-permute-start | bytes 786440 | tf_op jit(solution)/shard_map/ppermute | solution.py:13
  313.9 8.2 %collective-permute-done.10 = bf16[16,128,64]{1,2,0:T(8,128)(2,1)S(1)} collective-permute-done((bf16[16,128,64]{1,2,0:T(8,128)(2,1)S(1)}, bf16[16,128,64]{1,2,0:T(8,128)(2,1)S(1)}, u32[]{:S(2)}, u32[]{:S(2)}) %collective-permute-start.10) | collective-permute-done | bytes 262176 | tf_op jit(solution)/shard_map/ppermute | solution.py:13
  323.4 101.0 %while.25 = (s32[]{:T(128)}, bf16[16,512,64]{1,2,0:T(8,128)(2,1)S(1)}, s32[16]{0:T(128)S(1)}, f32[16,512,64]{1,2,0:T(8,128)}, bf16[512,16,11]{0,2,1:T(8,128)(2,1...) while((s32[]{:T(128)}, ...), condition=%wide.region_6.7_spmd.clone, body=%wide.region_4.6_spmd.sunk.clone | while | flops 50862084 | bytes 813239 | solution.py:157
  427.1 23.2 %all_to_all.69 = bf16[8,64,1024]{2,1,0:T(8,128)(2,1)S(1)} all-to-all(bf16[8,64,1024]{2,1,0:T(8,128)(2,1)S(1)} %copy.58), channel_id=1, replica_groups=mesh['ctx'=64,'head'=8] {'head'}, dimensions={0} | all-to-all | bytes 2097152 | tf_op jit(solution)/shard_map/all_to_all | solution.py:159
  (433 shorter events, 235.0 us)
Async XLA Ops:
  0.0 11.7 %copy-start = (bf16[64,1408]{1,0:T(8,128)(2,1)S(1)}, bf16[64,1408]{1,0:T(8,128)(2,1)}, u32[]{:S(2)}) copy-start(bf16[64,1408]{1,0:T(8,128)(2,1)} %param.16) | copy-start | bytes 540676
  1.6 28.2 %all-to-all-start.1 = ((bf16[8,2,512]{2,1,0:T(2,128)(2,1)}), bf16[8,2,512]{2,1,0:T(2,128)(2,1)S(1)}, u32[]{:S(2)}, u32[]{:S(2)}) async-start(bf16[8,2,512]{2,1,0:T(2,128)(2,1)} %reshape.222), calls=%async_computation.1 | async-start | bytes 32768 | tf_op jit(solution)/shard_map/all_to_all | solution.py:91
  26.2 44.1 %copy-start.3 = (bf16[512,128]{1,0:T(8,128)(2,1)}, bf16[512,128]{1,0:T(8,128)(2,1)S(1)}, u32[]{:S(2)}) copy-start(bf16[512,128]{1,0:T(8,128)(2,1)S(1)} %all_gather.3) | copy-start | bytes 393220
  26.2 3.5 copy-start.6
  30.4 9.1 %all-to-all-start.2 = ((bf16[8,64,128]{2,1,0:T(8,128)(2,1)}), bf16[8,64,128]{2,1,0:T(8,128)(2,1)S(1)}, u32[]{:S(2)}, u32[]{:S(2)}) async-start(bf16[8,64,128]{2,1,0:T(8,128)(2,1)} %stack.32), calls=%async_computation.2 | async-start | bytes 262144 | tf_op jit(solution)/shard_map/all_to_all | solution.py:95
  39.5 10.7 %all-to-all-start = ((bf16[64,8,176]{2,0,1:T(8,128)(2,1)}), bf16[64,8,176]{2,0,1:T(8,128)(2,1)S(1)}, u32[]{:S(2)}, u32[]{:S(2)}) async-start(bf16[64,8,176]{2,0,1:T(8,128)(2,1)} %copy.44), calls=%async_computation | async-start | bytes 524288 | tf_op jit(solution)/shard_map/all_to_all | solution.py:90
  43.9 10.7 %collective-permute-start.1 = (bf16[16]{0:T(256)(128)(2,1)S(1)}, bf16[16]{0:T(256)(128)(2,1)S(1)}, u32[]{:S(2)}, u32[]{:S(2)}) collective-permute-start(bf16[16]{0:T(256)(128)(2,1)S(1)} %convert_element_type.166), channel_id=1, source_target_pairs={{0,8},{8,0},{16,24},{24,16},{32,40},{40,32},{48,56},{56,48},{64,72... | collective-permute-start | bytes 104 | tf_op jit(solution)/shard_map/ppermute | solution.py:13
  50.2 21.8 %all-to-all-start.3 = ((bf16[64,8,1024]{2,0,1:T(8,128)(2,1)}), bf16[64,8,1024]{2,0,1:T(8,128)(2,1)S(1)}, u32[]{:S(2)}, u32[]{:S(2)}) async-start(bf16[64,8,1024]{2,0,1:T(8,128)(2,1)} %bitcast.123), calls=%async_computation.3 | async-start | bytes 2097152 | tf_op jit(solution)/shard_map/all_to_all | solution.py:89
  54.7 5.5 %collective-permute-start.3 = (bf16[16]{0:T(256)(128)(2,1)S(1)}, bf16[16]{0:T(256)(128)(2,1)S(1)}, u32[]{:S(2)}, u32[]{:S(2)}) collective-permute-start(bf16[16]{0:T(256)(128)(2,1)S(1)} %fusion.63), channel_id=1, source_target_pairs={{0,16},{8,24},{16,0},{24,8},{32,48},{40,56},{48,32},{56,40},{64,80... | collective-permute-start | bytes 104 | tf_op jit(solution)/shard_map/ppermute | solution.py:13
  60.2 8.2 %collective-permute-start.5 = (bf16[16]{0:T(256)(128)(2,1)S(1)}, bf16[16]{0:T(256)(128)(2,1)S(1)}, u32[]{:S(2)}, u32[]{:S(2)}) collective-permute-start(bf16[16]{0:T(256)(128)(2,1)S(1)} %convert_element_type.176), channel_id=1, source_target_pairs={{0,32},{8,40},{16,48},{24,56},{32,0},{40,8},{48,16},{56,24},{64,96... | collective-permute-start | bytes 104 | tf_op jit(solution)/shard_map/ppermute | solution.py:13
  68.4 171.3 %collective-permute-start.7 = (bf16[16]{0:T(256)(128)(2,1)S(1)}, bf16[16]{0:T(256)(128)(2,1)S(1)}, u32[]{:S(2)}, u32[]{:S(2)}) collective-permute-start(bf16[16]{0:T(256)(128)(2,1)S(1)} %convert_element_type.181), channel_id=1, source_target_pairs={{0,64},{8,72},{16,80},{24,88},{32,96},{40,104},{48,112},{56,120},{... | collective-permute-start | bytes 104 | tf_op jit(solution)/shard_map/ppermute | solution.py:13
  71.9 1.0 copy-start.2
  236.7 25.7 %copy-start.1 = (f32[16,128,64]{1,2,0:T(8,128)S(1)}, f32[16,128,64]{1,2,0:T(8,128)}, u32[]{:S(2)}) copy-start(f32[16,128,64]{1,2,0:T(8,128)} %get-tuple-element.111) | copy-start | bytes 1572868
  236.7 32.6 %copy-start.7 = (f32[128]{0:T(128)S(1)}, f32[128]{0:T(128)}, u32[]{:S(2)}) copy-start(f32[128]{0:T(128)} %param.17) | copy-start | bytes 1540
  237.8 7.8 %collective-permute-start = (bf16[16,128,64]{1,2,0:T(8,128)(2,1)S(1)}, bf16[16,128,64]{1,2,0:T(8,128)(2,1)S(1)}, u32[]{:S(2)}, u32[]{:S(2)}) collective-permute-start(bf16[16,128,64]{1,2,0:T(8,128)(2,1)S(1)} %convert_element_type.163), channel_id=1, source_target_pairs={{0,8},{8,0},{16,24},{24,16},{32,40},{40,32},{48,56},{56,48},{64,72... | collective-permute-start | bytes 786440 | tf_op jit(solution)/shard_map/ppermute | solution.py:13
  239.8 5.8 %collective-permute-start.9 = (bf16[16]{0:T(256)(128)(2,1)S(1)}, bf16[16]{0:T(256)(128)(2,1)S(1)}, u32[]{:S(2)}, u32[]{:S(2)}) collective-permute-start(bf16[16]{0:T(256)(128)(2,1)S(1)} %get-tuple-element.258), channel_id=1, source_target_pairs={{0,128},{8,136},{16,144},{24,152},{32,160},{40,168},{48,176},{56,1... | collective-permute-start | bytes 104 | tf_op jit(solution)/shard_map/ppermute | solution.py:13
  246.9 15.5 %collective-permute-start.2 = (bf16[16,128,64]{1,2,0:T(8,128)(2,1)S(1)}, bf16[16,128,64]{1,2,0:T(8,128)(2,1)S(1)}, u32[]{:S(2)}, u32[]{:S(2)}) collective-permute-start(bf16[16,128,64]{1,2,0:T(8,128)(2,1)S(1)} %fusion.68), channel_id=1, source_target_pairs={{0,16},{8,24},{16,0},{24,8},{32,48},{40,56},{48,32},{56,40},{64,80... | collective-permute-start | bytes 786440 | tf_op jit(solution)/shard_map/ppermute | solution.py:13
  262.7 18.1 %collective-permute-start.4 = (bf16[16,128,64]{1,2,0:T(8,128)(2,1)S(1)}, bf16[16,128,64]{1,2,0:T(8,128)(2,1)S(1)}, u32[]{:S(2)}, u32[]{:S(2)}) collective-permute-start(bf16[16,128,64]{1,2,0:T(8,128)(2,1)S(1)} %fusion.67), channel_id=1, source_target_pairs={{0,32},{8,40},{16,48},{24,56},{32,0},{40,8},{48,16},{56,24},{64,96... | collective-permute-start | bytes 786440 | tf_op jit(solution)/shard_map/ppermute | solution.py:13
  281.3 7.7 %collective-permute-start.6 = (bf16[16,128,64]{1,2,0:T(8,128)(2,1)S(1)}, bf16[16,128,64]{1,2,0:T(8,128)(2,1)S(1)}, u32[]{:S(2)}, u32[]{:S(2)}) collective-permute-start(bf16[16,128,64]{1,2,0:T(8,128)(2,1)S(1)} %get-tuple-element.253), channel_id=1, source_target_pairs={{0,64},{8,72},{16,80},{24,88},{32,96},{40,104},{48,112},{56,120},{... | collective-permute-start | bytes 786440 | tf_op jit(solution)/shard_map/ppermute | solution.py:13
  289.2 15.2 %collective-permute-start.8 = (bf16[16,128,64]{1,2,0:T(8,128)(2,1)S(1)}, bf16[16,128,64]{1,2,0:T(8,128)(2,1)S(1)}, u32[]{:S(2)}, u32[]{:S(2)}) collective-permute-start(bf16[16,128,64]{1,2,0:T(8,128)(2,1)S(1)} %fusion.66), channel_id=1, source_target_pairs={{0,128},{8,136},{16,144},{24,152},{32,160},{40,168},{48,176},{56,1... | collective-permute-start | bytes 786440 | tf_op jit(solution)/shard_map/ppermute | solution.py:13
  293.6 29.9 %copy-start.4 = (bf16[512,128]{1,0:T(8,128)(2,1)S(1)}, bf16[512,128]{1,0:T(8,128)(2,1)}, u32[]{:S(2)}) copy-start(bf16[512,128]{1,0:T(8,128)(2,1)} %copy-done.3) | copy-start | bytes 393220
  304.7 17.4 %collective-permute-start.10 = (bf16[16,128,64]{1,2,0:T(8,128)(2,1)S(1)}, bf16[16,128,64]{1,2,0:T(8,128)(2,1)S(1)}, u32[]{:S(2)}, u32[]{:S(2)}) collective-permute-start(bf16[16,128,64]{1,2,0:T(8,128)(2,1)S(1)} %fusion.42), channel_id=1, source_target_pairs={{0,256},{8,264},{16,272},{24,280},{32,288},{40,296},{48,304},{56,3... | collective-permute-start | bytes 786440 | tf_op jit(solution)/shard_map/ppermute | solution.py:13
  322.3 1.1 copy-start.5
